TPU v7x, 32 devices: a whole 2x2x4 slice. The times are simulated.
32 devices in a mesh: face: 8 (over y, x, core), member: 4 (over z).
Axes of the slice: x: 2, y: 2, z: 4, core: 2. Of those that a mesh axis runs over, the one named last changes fastest.
Arguments:
- features: bfloat16 [8, 48, 16, 16, 256], P('member', 'face'), may hold values from -6 to 6
- observed: bfloat16 [48, 80, 256], P('face', None, 'member'), may hold values from -6 to 6
- conv_weights: bfloat16 [2304, 2, 256], P(('face', 'member')), may hold values from -0.125 to 0.125
- head_weight: bfloat16 [256, 80], P(('face', 'member')), may hold values from -0.375 to 0.375
- adjacency: int32 [48, 4, 3], replicated, may hold values from 0 to 47, as said below
- placement_map: int32 [48], replicated, may hold values from 0 to 47, each once
Outputs:
- conv_grads: float32 [2304, 2, 256], P(('face', 'member'))
- head_grad: float32 [256, 80], P(('face', 'member'))
Inputs may be any that keep to these rules, and one draw needn't show every extreme that they name: `adjacency`: the table is the gluing of the 12 HEALPix base faces, each cut into 4 square tiles, under a labelling of the tiles drawn from the seed: entry [t, a] = (n, b, f) glues side a of tile t to side b of tile n, reversed when f is 1; the gluing is mutual (entry [n, b] is (t, a, f)) and never joins a side to itself. `placement_map`: each tile stands at exactly one slot.
All inputs are finite; a program needn't handle non-finite values.
Results may differ from a plain program's by a relative error of at most 0.0005.
Values may be sent and summed in bfloat16 or wider, within the bound.
A program may use at most 128 MiB of HBM per device.

v0:
```python
import jax
import jax.numpy as jnp
from jax import lax
from jax.sharding import PartitionSpec as P

smooth_sq = 0.0625


def split_edges(grid_field):
    return jnp.stack(
        [
            grid_field[:, :, 0],
            grid_field[:, :, :, -1],
            grid_field[:, :, -1],
            grid_field[:, :, :, 0],
        ],
        axis=2,
    )


def border_of(padded):
    return jnp.stack(
        [
            padded[:, :, 0, 1:-1],
            padded[:, :, 1:-1, -1],
            padded[:, :, -1, 1:-1],
            padded[:, :, 1:-1, 0],
        ],
        axis=2,
    )


def surround(grid_field, border):
    ensemble_members, tile_count, height, tile_w, channels = grid_field.shape
    corner = jnp.zeros((ensemble_members, tile_count, 1, 1, channels), grid_field.dtype)
    top_row = jnp.concatenate([corner, border[:, :, 0][:, :, None], corner], axis=3)
    low_row = jnp.concatenate([corner, border[:, :, 2][:, :, None], corner], axis=3)
    middle = jnp.concatenate(
        [border[:, :, 3][:, :, :, None], grid_field, border[:, :, 1][:, :, :, None]], axis=3
    )
    return jnp.concatenate([top_row, middle, low_row], axis=2)


def convolve(padded, weight):
    channels = weight.shape[1]
    height = padded.shape[2] - 2
    tile_w = padded.shape[3] - 2
    summed = None
    for tap_index in range(9):
        row_off, col_off = divmod(tap_index, 3)
        window = padded[:, :, row_off : row_off + height, col_off : col_off + tile_w, :]
        product_part = jnp.dot(
            window.reshape(-1, channels),
            weight[tap_index * channels : (tap_index + 1) * channels],
            preferred_element_type=jnp.float32,
        )
        summed = product_part if summed is None else summed + product_part
    return summed.reshape(padded.shape[:2] + (height, tile_w, channels))


def transpose_conv(slope_in, weight):
    channels = weight.shape[1]
    ensemble_members, tile_count, height, tile_w, _ = slope_in.shape
    result = jnp.zeros(
        (ensemble_members, tile_count, height + 2, tile_w + 2, channels), jnp.float32
    )
    flat_slope = slope_in.reshape(-1, channels)
    for tap_index in range(9):
        row_off, col_off = divmod(tap_index, 3)
        product_part = lax.dot_general(
            flat_slope,
            weight[tap_index * channels : (tap_index + 1) * channels],
            (((1,), (1,)), ((), ())),
            preferred_element_type=jnp.float32,
        )
        result = result.at[:, :, row_off : row_off + height, col_off : col_off + tile_w, :].add(
            product_part.reshape(slope_in.shape)
        )
    return result


def weight_slope(padded, slope_in):
    channels = slope_in.shape[-1]
    height = slope_in.shape[2]
    tile_w = slope_in.shape[3]
    flat_slope = slope_in.reshape(-1, channels)
    pieces_out = []
    for tap_index in range(9):
        row_off, col_off = divmod(tap_index, 3)
        window = padded[:, :, row_off : row_off + height, col_off : col_off + tile_w, :]
        pieces_out.append(
            lax.dot_general(
                window.reshape(-1, channels),
                flat_slope,
                (((0,), (0,)), ((), ())),
                preferred_element_type=jnp.float32,
            )
        )
    return jnp.concatenate(pieces_out, axis=0)


def dsilu(argument):
    sigmoid_v = jax.nn.sigmoid(argument)
    return sigmoid_v * (1.0 + argument * (1.0 - sigmoid_v))


def partner_table(adjacency, placement_map, first_slot, tile_dev):
    tile_count = placement_map.shape[0]
    slot_ids = jnp.arange(tile_count, dtype=jnp.int32)
    my_slots = first_slot + jnp.arange(tile_dev, dtype=jnp.int32)
    slot_hit = (slot_ids[None, :] == my_slots[:, None]).astype(jnp.int32)
    my_tiles = jnp.sum(slot_hit * placement_map[None, :], axis=1)
    tile_hit = (slot_ids[None, :] == my_tiles[:, None]).astype(jnp.int32)
    entries = jnp.sum(tile_hit[:, :, None, None] * adjacency[None], axis=1)
    slot_of = jnp.sum(
        slot_ids[:, None] * (placement_map[:, None] == slot_ids[None, :]).astype(jnp.int32), axis=0
    )
    source_slot = jnp.sum(
        (slot_ids[None, None, :] == entries[:, :, 0][:, :, None]).astype(jnp.int32)
        * slot_of[None, None, :],
        axis=2,
    )
    source_index = source_slot * 4 + entries[:, :, 1]
    edge_ids = jnp.arange(tile_count * 4, dtype=jnp.int32)
    selector = (edge_ids[None, None, :] == source_index[:, :, None]).astype(jnp.bfloat16)
    return (selector, entries[:, :, 2])


def fetch_rims(gathered, selector, flip_flags, tile_dev):
    ensemble_members, tile_count, side_count, length, channels = gathered.shape
    flattened = gathered.reshape(ensemble_members, tile_count * side_count, length * channels)
    fetched = jnp.einsum("abe,mef->mabf", selector, flattened, preferred_element_type=jnp.float32)
    fetched = fetched.astype(jnp.bfloat16).reshape(
        ensemble_members, tile_dev, side_count, length, channels
    )
    return jnp.where(flip_flags[None, :, :, None, None] == 1, fetched[:, :, :, ::-1, :], fetched)


def score_slope(local_vals, all_vals, obs_vals, height):
    ensemble_members = all_vals.shape[0]
    spread = local_vals[:, None] - all_vals[None]
    paired = jnp.sum(spread * lax.rsqrt(spread * spread + smooth_sq), axis=1)
    own_gap = local_vals - obs_vals[None]
    return (
        own_gap * lax.rsqrt(own_gap * own_gap + smooth_sq) / ensemble_members
        - paired / (ensemble_members * ensemble_members)
    ) / height


def shards(features, observed, conv_weights, head_weight, adjacency, placement_map):
    members, tile_dev, height, tile_w, channels = features.shape
    full_weights, full_head = (
        lax.all_gather(conv_weights, ("face", "member"), axis=0, tiled=True),
        lax.all_gather(head_weight, ("face", "member"), axis=0, tiled=True),
    )
    selector, flip_flags = partner_table(
        adjacency, placement_map, lax.axis_index("face") * tile_dev, tile_dev
    )
    feature_edges = lax.all_gather(split_edges(features), "face", axis=1, tiled=True)
    pad_in = surround(features, fetch_rims(feature_edges, selector, flip_flags, tile_dev))
    pre_one = convolve(pad_in, full_weights[:, 0, :])
    act_one = jax.nn.silu(pre_one).astype(jnp.bfloat16)
    hidden_edges = lax.all_gather(split_edges(act_one), "face", axis=1, tiled=True)
    pad_mid = surround(act_one, fetch_rims(hidden_edges, selector, flip_flags, tile_dev))
    pre_two = convolve(pad_mid, full_weights[:, 1, :])
    act_two = jax.nn.silu(pre_two).astype(jnp.bfloat16)
    flat_two = act_two.reshape(members, tile_dev, height * tile_w, channels)
    outputs = jnp.einsum(
        "mtpc,cv->mtvp", flat_two, full_head, preferred_element_type=jnp.float32
    ).astype(jnp.bfloat16)
    by_pixel = lax.all_to_all(outputs, "member", split_axis=3, concat_axis=0, tiled=True)
    pixel_vals = by_pixel.astype(jnp.float32)
    slope_cells = score_slope(pixel_vals, pixel_vals, observed.astype(jnp.float32), height).astype(
        jnp.bfloat16
    )
    slope_out = lax.all_to_all(slope_cells, "member", split_axis=0, concat_axis=3, tiled=True)
    head_term = jnp.einsum("mtpc,mtvp->cv", flat_two, slope_out, preferred_element_type=jnp.float32)
    back_two = jnp.einsum("mtvp,cv->mtpc", slope_out, full_head, preferred_element_type=jnp.float32)
    back_two = back_two.reshape(members, tile_dev, height, tile_w, channels)
    slope_two = (back_two * dsilu(pre_two)).astype(jnp.bfloat16)
    grad_two = weight_slope(pad_mid, slope_two)
    late_shard, head_shard = (
        lax.psum_scatter(grad_two, ("face", "member"), scatter_dimension=0, tiled=True),
        lax.psum_scatter(head_term, ("face", "member"), scatter_dimension=0, tiled=True),
    )
    pad_slope = transpose_conv(slope_two, full_weights[:, 1, :]).astype(jnp.bfloat16)
    rim_edges = lax.all_gather(border_of(pad_slope), "face", axis=1, tiled=True)
    returned = fetch_rims(rim_edges, selector, flip_flags, tile_dev).astype(jnp.float32)
    slope_mid = pad_slope[:, :, 1:-1, 1:-1].astype(jnp.float32)
    slope_mid = slope_mid.at[:, :, 0].add(returned[:, :, 0])
    slope_mid = slope_mid.at[:, :, :, -1].add(returned[:, :, 1])
    slope_mid = slope_mid.at[:, :, -1].add(returned[:, :, 2])
    slope_mid = slope_mid.at[:, :, :, 0].add(returned[:, :, 3])
    slope_one = (slope_mid * dsilu(pre_one)).astype(jnp.bfloat16)
    grad_one = weight_slope(pad_in, slope_one)
    early_shard = lax.psum_scatter(grad_one, ("face", "member"), scatter_dimension=0, tiled=True)
    conv_shard = jnp.stack([early_shard, late_shard], axis=1)
    return (conv_shard, head_shard)


def solution(mesh):
    in_specs = (
        P("member", "face", None, None, None),
        P("face", None, "member"),
        P(("face", "member"), None, None),
        P(("face", "member"), None),
        P(),
        P(),
    )
    out_specs = (P(("face", "member"), None, None), P(("face", "member"), None))
    return jax.shard_map(shards, mesh=mesh, in_specs=in_specs, out_specs=out_specs, check_vma=False)
```

profile of v0, /device:TPU:0, one launch (start us, length us, event | category | flops | bytes accessed | tf_op | source)
XLA Modules:
  0.0 850.0 jit_solution(15067462551593991296)
XLA Ops:
  7.2 1.8 fusion.111
  13.3 32.6 %all-gather.5.cloned.1.call-done = bf16[2,48,4,16,256]{4,3,1,0,2:T(8,128)(2,1)} async-done(((bf16[2,6,4,16,256]{4,3,1,0,2:T(8,128)(2,1)}), bf16[2,48,4,16,256]{4,3,1,0,2:T(8,128)(2,1)}) %all-gather.5.cloned.1.call-update) | async-done | bytes 3145744 | tf_op jit(solution)/shard_map/all_gather | solution.py:159
  45.9 2.3 copy.300
  48.3 3.4 reshape.811
  51.7 2.6 fusion.3
  57.0 2.9 pad_maximum_fusion.4
  60.0 3.6 pad_maximum_fusion
  63.6 3.6 fusion.108
  67.3 3.2 fusion.107
  70.5 36.2 %all-gather.7.cloned.1.call-done = bf16[2304,2,256]{2,0,1:T(8,128)(2,1)} async-done(((bf16[72,2,256]{2,0,1:T(8,128)(2,1)}), bf16[2304,2,256]{2,0,1:T(8,128)(2,1)}) %all-gather.7.cloned.1.call-update) | async-done | bytes 2359312 | tf_op jit(solution)/shard_map/all_gather | solution.py:153
  106.7 2.1 fusion.32
  110.4 1.6 convolution_add_fusion.14
  115.0 1.6 convolution_add_fusion.11
  118.3 1.6 convolution_add_fusion.9
  124.4 67.0 %all_gather.18 = bf16[256,80]{1,0:T(8,128)(2,1)S(1)} all-gather(bf16[8,80]{1,0:T(8,128)(2,1)S(1)} %copy-done.36), channel_id=1, replica_groups=mesh['face'=8,'member'=4] {'face','member'}, dimensions={0}, use_global_device_ids=true | all-gather | bytes 42240 | tf_op jit(solution)/shard_map/all_gather | solution.py:154
  191.4 6.1 reshape.813
  197.5 2.6 fusion.4
  204.4 3.9 pad_maximum_fusion.1
  218.7 2.4 convolution_add_fusion
  221.0 3.5 copy.327
  224.6 2.7 multiply_convert_fusion.2
  228.9 1.9 copy.329
  230.8 3.5 all-to-all-start
  234.3 16.0 %all-to-all-done = bf16[2,6,80,256]{2,0,1,3:T(2,128)(2,1)S(1)} async-done(((bf16[2,6,80,256]{2,0,1,3:T(2,128)(2,1)}), bf16[2,6,80,256]{2,0,1,3:T(2,128)(2,1)S(1)}, u32[]{:S(2)}, u32[]{:S(2)}) %all-to-all-start) | async-done | bytes 491552 | tf_op jit(solution)/shard_map/all_to_all | solution.py:171
  250.8 3.1 fusion.2
  255.3 3.5 all-to-all-start.1
  261.1 14.9 %all-to-all-done.1 = bf16[8,6,80,64]{2,3,1,0:T(8,128)(2,1)S(1)} async-done(((bf16[8,6,80,64]{2,3,1,0:T(8,128)(2,1)}), bf16[8,6,80,64]{2,3,1,0:T(8,128)(2,1)S(1)}, u32[]{:S(2)}, u32[]{:S(2)}) %all-to-all-start.1) | async-done | bytes 491552 | tf_op jit(solution)/shard_map/all_to_all | solution.py:176
  276.0 3.5 multiply_convert_fusion.1
  282.5 3.0 scatter-add.44
  285.5 4.8 dynamic-slice_add_fusion
  290.3 18.3 %scatter-add.45 = f32[2,6,18,18,256]{4,2,3,1,0:T(8,128)} dynamic-update-slice(f32[2,6,18,18,256]{4,2,3,1,0:T(8,128)} %scatter-add.44, f32[2,6,16,16,256]{4,2,3,1,0:T(8,128)} %dynamic-slice_add_fusion, s32[]{:T(128)} %constant.394.clone.1, s32[]{:T(128)} %constant.394.clone.1, s32[]{:T(128)} %bitcast.74, s32[]{:T(128)} %bitcast.75, s32[]{:T(128)} %constant.394.clone.1) | dynamic-update-slice | bytes 6291460 | tf_op jit(solution)/shard_map/scatter-add | solution.py:76
  308.5 7.0 add_select_fusion
  315.5 18.3 %scatter-add.46 = f32[2,6,18,18,256]{4,2,3,1,0:T(8,128)} dynamic-update-slice(f32[2,6,18,18,256]{4,2,3,1,0:T(8,128)} %scatter-add.45, f32[2,6,16,16,256]{4,2,3,1,0:T(8,128)} %add_select_fusion, s32[]{:T(128)} %constant.394.clone.1, s32[]{:T(128)} %constant.394.clone.1, s32[]{:T(128)} %bitcast.78, s32[]{:T(128)} %bitcast.79, s32[]{:T(128)} %constant.394.clone.1) | dynamic-update-slice | bytes 6291460 | tf_op jit(solution)/shard_map/scatter-add | solution.py:76
  333.8 5.0 slice_add_fusion.5
  338.7 17.0 %scatter-add.49 = f32[2,6,18,18,256]{4,2,3,1,0:T(8,128)} dynamic-update-slice(f32[2,6,18,18,256]{4,2,3,1,0:T(8,128)} %scatter-add.46, f32[2,6,16,16,256]{4,2,3,1,0:T(8,128)} %slice_add_fusion.5, s32[]{:T(128)} %constant.394.clone.1, s32[]{:T(128)} %constant.394.clone.1, s32[]{:T(128)} %constant.395.clone.1, s32[]{:T(128)} %constant.394.clone.1, s32[]{:T(128)} %constant.394.clone.1) | dynamic-update-slice | bytes 6291460 | tf_op jit(solution)/shard_map/scatter-add | solution.py:76
  355.7 5.0 slice_add_fusion.4
  360.6 16.9 %scatter-add.50 = f32[2,6,18,18,256]{4,2,3,1,0:T(8,128)} dynamic-update-slice(f32[2,6,18,18,256]{4,2,3,1,0:T(8,128)} %scatter-add.49, f32[2,6,16,16,256]{4,2,3,1,0:T(8,128)} %slice_add_fusion.4, s32[]{:T(128)} %constant.394.clone.1, s32[]{:T(128)} %constant.394.clone.1, s32[]{:T(128)} %constant.395.clone.1, s32[]{:T(128)} %constant.395.clone.1, s32[]{:T(128)} %constant.394.clone.1) | dynamic-update-slice | bytes 6291460 | tf_op jit(solution)/shard_map/scatter-add | solution.py:76
  377.6 5.0 slice_add_fusion.3
  382.5 16.9 %scatter-add.51 = f32[2,6,18,18,256]{4,2,3,1,0:T(8,128)} dynamic-update-slice(f32[2,6,18,18,256]{4,2,3,1,0:T(8,128)} %scatter-add.50, f32[2,6,16,16,256]{4,2,3,1,0:T(8,128)} %slice_add_fusion.3, s32[]{:T(128)} %constant.394.clone.1, s32[]{:T(128)} %constant.394.clone.1, s32[]{:T(128)} %constant.395.clone.1, s32[]{:T(128)} %constant.403.clone.1, s32[]{:T(128)} %constant.394.clone.1) | dynamic-update-slice | bytes 6291460 | tf_op jit(solution)/shard_map/scatter-add | solution.py:76
  399.5 5.0 slice_add_fusion.2
  404.4 17.0 %scatter-add.54 = f32[2,6,18,18,256]{4,2,3,1,0:T(8,128)} dynamic-update-slice(f32[2,6,18,18,256]{4,2,3,1,0:T(8,128)} %scatter-add.51, f32[2,6,16,16,256]{4,2,3,1,0:T(8,128)} %slice_add_fusion.2, s32[]{:T(128)} %constant.394.clone.1, s32[]{:T(128)} %constant.394.clone.1, s32[]{:T(128)} %constant.403.clone.1, s32[]{:T(128)} %constant.394.clone.1, s32[]{:T(128)} %constant.394.clone.1) | dynamic-update-slice | bytes 6291460 | tf_op jit(solution)/shard_map/scatter-add | solution.py:76
  421.4 5.0 slice_add_fusion.1
  426.4 16.9 %scatter-add.55 = f32[2,6,18,18,256]{4,2,3,1,0:T(8,128)} dynamic-update-slice(f32[2,6,18,18,256]{4,2,3,1,0:T(8,128)} %scatter-add.54, f32[2,6,16,16,256]{4,2,3,1,0:T(8,128)} %slice_add_fusion.1, s32[]{:T(128)} %constant.394.clone.1, s32[]{:T(128)} %constant.394.clone.1, s32[]{:T(128)} %constant.403.clone.1, s32[]{:T(128)} %constant.395.clone.1, s32[]{:T(128)} %constant.394.clone.1) | dynamic-update-slice | bytes 6291460 | tf_op jit(solution)/shard_map/scatter-add | solution.py:76
  443.3 5.0 slice_add_fusion
  448.3 16.9 %scatter-add.56 = f32[2,6,18,18,256]{4,2,3,1,0:T(8,128)} dynamic-update-slice(f32[2,6,18,18,256]{4,2,3,1,0:T(8,128)} %scatter-add.55, f32[2,6,16,16,256]{4,2,3,1,0:T(8,128)} %slice_add_fusion, s32[]{:T(128)} %constant.394.clone.1, s32[]{:T(128)} %constant.394.clone.1, s32[]{:T(128)} %constant.403.clone.1, s32[]{:T(128)} %constant.403.clone.1, s32[]{:T(128)} %constant.394.clone.1) | dynamic-update-slice | bytes 6291460 | tf_op jit(solution)/shard_map/scatter-add | solution.py:76
  465.2 2.9 convert_element_type.103
  471.1 2.8 convolution_bitcast_fusion.18
  473.9 3.1 fusion.17
  485.7 3.9 slice_convert_fusion
  489.7 13.1 %all-gather.11.cloned.1.call-done = bf16[2,48,4,16,256]{4,3,1,0,2:T(8,128)(2,1)} async-done(((bf16[2,6,4,16,256]{4,3,1,0,2:T(8,128)(2,1)}), bf16[2,48,4,16,256]{4,3,1,0,2:T(8,128)(2,1)}) %all-gather.11.cloned.1.call-update) | async-done | bytes 3145744 | tf_op jit(solution)/shard_map/all_gather | solution.py:187
  502.8 2.3 copy.345
  505.2 3.4 reshape.825
  508.6 2.6 fusion.5
  512.3 2.1 fusion.112
  514.4 5.4 scatter-add.59
  519.9 1.6 fusion.31
  521.5 1.7 slice_add_fusion.6
  523.3 5.5 scatter-add.61
  528.7 5.9 copy.351
  537.1 5.6 scatter-add.64
  542.7 3.1 multiply_convert_fusion
  556.4 76.9 %all-reduce.4.cloned.1.call-done = f32[256,80]{1,0:T(8,128)} async-done(((f32[256,80]{1,0:T(8,128)}), f32[256,80]{1,0:T(8,128)}) %all-reduce.4.cloned.1.call-update) | async-done | bytes 81936
  634.6 102.5 %reduce-scatter.5.cloned.1.call-done = f32[72,256]{1,0:T(8,128)} async-done(((f32[2304,256]{1,0:T(8,128)}), f32[72,256]{1,0:T(8,128)}) %reduce-scatter.5.cloned.1.call-update) | async-done | bytes 73744 | tf_op jit(solution)/shard_map/reduce_scatter | solution.py:183
  737.1 103.9 %reduce-scatter.3.cloned.1.call-done = f32[72,256]{1,0:T(8,128)} async-done(((f32[2304,256]{1,0:T(8,128)}), f32[72,256]{1,0:T(8,128)}) %reduce-scatter.3.cloned.1.call-update) | async-done | bytes 73744 | tf_op jit(solution)/shard_map/reduce_scatter | solution.py:196
  (193 shorter events, 69.2 us)
Async XLA Ops:
  7.2 3.7 copy-start.34
  7.2 4.5 copy-start.38
  7.2 4.8 copy-start.35
  7.2 38.7 %all-gather.5.cloned.1.call-start = ((), (), s32[]{:S(2)}) async-start(), calls=%async_computation.4 | async-start | bytes 3538944 | tf_op jit(solution)/shard_map/all_gather | solution.py:159
  10.8 95.9 %all-gather.7.cloned.1.call-start = ((), (), s32[]{:S(2)}) async-start(), calls=%async_computation.5 | async-start | bytes 2433024 | tf_op jit(solution)/shard_map/all_gather | solution.py:153
  11.6 179.8 %all-gather.9.cloned.1.call-start = ((), (), s32[]{:S(2)}) async-start(), calls=%async_computation.6 | async-start | bytes 3538944 | tf_op jit(solution)/shard_map/all_gather | solution.py:163
  54.8 2.2 copy-start.13
  60.0 55.0 %copy-start.15 = (bf16[2,6,16,16,256]{4,3,2,1,0:T(8,128)(2,1)}, bf16[2,6,16,16,256]{4,3,2,1,0:T(8,128)(2,1)S(1)}, u32[]{:S(2)}) copy-start(bf16[2,6,16,16,256]{4,3,2,1,0:T(8,128)(2,1)S(1)} %get-tuple-element.196) | copy-start | bytes 4718596
  63.6 3.7 copy-start.8
  63.6 3.7 copy-start
  106.7 2.1 copy-start.28
  108.8 1.6 copy-start.27
  110.4 1.6 copy-start.17
  115.0 1.6 copy-start.26
  116.6 1.6 copy-start.25
  118.2 1.6 copy-start.24
  121.4 1.6 copy-start.4
  123.0 1.4 copy-start.36
  204.4 9.6 %copy-start.21 = (bf16[2,6,16,16,256]{4,3,2,1,0:T(8,128)(2,1)}, bf16[2,6,16,16,256]{4,3,2,1,0:T(8,128)(2,1)S(1)}, u32[]{:S(2)}) copy-start(bf16[2,6,16,16,256]{4,3,2,1,0:T(8,128)(2,1)S(1)} %get-tuple-element.191) | copy-start | bytes 4718596
  204.4 12.5 %copy-start.19 = (bf16[2,6,16,16,256]{4,3,2,1,0:T(8,128)(2,1)}, bf16[2,6,16,16,256]{4,3,2,1,0:T(8,128)(2,1)S(1)}, u32[]{:S(2)}) copy-start(bf16[2,6,16,16,256]{4,3,2,1,0:T(8,128)(2,1)S(1)} %get-tuple-element.190) | copy-start | bytes 4718596
  208.3 1.5 copy-start.10
  208.3 2.2 copy-start.2
  210.5 1.7 copy-start.29
  214.0 1.9 copy-start.5
  227.3 1.2 copy-start.7
  228.5 5.8 copy-start.33
  230.8 19.5 %all-to-all-start = ((bf16[2,6,80,256]{2,0,1,3:T(2,128)(2,1)}), bf16[2,6,80,256]{2,0,1,3:T(2,128)(2,1)S(1)}, u32[]{:S(2)}, u32[]{:S(2)}) async-start(bf16[2,6,80,256]{2,0,1,3:T(2,128)(2,1)} %copy.329), calls=%async_computation | async-start | bytes 1572864 | tf_op jit(solution)/shard_map/all_to_all | solution.py:171
  253.9 6.4 copy-start.37
  255.3 20.7 %all-to-all-start.1 = ((bf16[8,6,80,64]{2,3,1,0:T(8,128)(2,1)}), bf16[8,6,80,64]{2,3,1,0:T(8,128)(2,1)S(1)}, u32[]{:S(2)}, u32[]{:S(2)}) async-start(bf16[8,6,80,64]{2,3,1,0:T(8,128)(2,1)} %multiply_convert_fusion.6), calls=%async_computation.1 | async-start | bytes 1572864 | tf_op jit(solution)/shard_map/all_to_all | solution.py:176
  258.8 244.0 %all-gather.11.cloned.1.call-start = ((), (), s32[]{:S(2)}) async-start(), calls=%async_computation.7 | async-start | bytes 3538944 | tf_op jit(solution)/shard_map/all_gather | solution.py:187
  276.0 3.5 copy-start.30
  276.0 3.5 copy-start.11
  465.2 3.4 copy-start.12
  468.1 1.8 copy-start.23
  470.8 162.4 %all-reduce.4.cloned.1.call-start = ((), (), s32[]{:S(2)}) async-start(), calls=%async_computation.10 | async-start | bytes 262144
  473.9 3.1 copy-start.22
  478.4 1.5 copy-start.20
  479.9 1.8 copy-start.3
  485.6 251.4 %reduce-scatter.5.cloned.1.call-start = ((), (), s32[]{:S(2)}) async-start(), calls=%async_computation.9 | async-start | bytes 2433024 | tf_op jit(solution)/shard_map/reduce_scatter | solution.py:183
  489.6 351.4 %reduce-scatter.3.cloned.1.call-start = ((), (), s32[]{:S(2)}) async-start(), calls=%async_computation.8 | async-start | bytes 2433024 | tf_op jit(solution)/shard_map/reduce_scatter | solution.py:196
  512.3 10.9 %copy-start.31 = (f32[2,6,4,16,256]{4,2,3,1,0:T(4,128)}, f32[2,6,4,16,256]{4,2,3,1,0:T(4,128)S(1)}, u32[]{:S(2)}) copy-start(f32[2,6,4,16,256]{4,2,3,1,0:T(4,128)S(1)} %fusion.29) | copy-start | bytes 2359300
  528.7 14.0 %copy-start.6 = (f32[3072,256]{1,0:T(8,128)S(1)}, f32[3072,256]{1,0:T(8,128)}, u32[]{:S(2)}) copy-start(f32[3072,256]{1,0:T(8,128)} %copy-done.4) | copy-start | bytes 9437188
  542.7 3.1 copy-start.9
  547.1 1.4 copy-start.18
  548.5 1.4 copy-start.14
  549.9 1.4 copy-start.16
  551.4 1.7 copy-start.1
  555.0 1.4 copy-start.32
Sparse Core Ops, SparseCore 0:
  11.0 34.8 all-gather.4
  49.5 57.1 all-gather.6
  124.5 31.0 all-gather.8
  471.0 31.8 all-gather.10
  508.8 124.4 all-reduce.3
  638.4 98.5 reduce-scatter.4
  742.3 98.6 reduce-scatter.2
where the time goes:
time: 861 us; the launch traced here: 850 us
  waiting for transfers between devices  396 us (46%)
  local copies, waits for them, and re-layouts  220 us (26%)
  matrix products  99.1 us (12%)
  blocking collectives  67 us (8%)
  other arithmetic  44.6 us (5%)
  between operations  15.6 us (2%)
    scatter-add x9, local copies, waits for them, and re-layouts, transpose_conv(): result.at[:, :, row_off:row_off + height, col_off:col_off + tile_w, :]  141 us
    reduce_scatter x1, waiting for transfers between devices, shards(): lax.psum_scatter(grad_one, ('face', 'member'), scatter_dimension=0, tiled...  104 us
    reduce_scatter x1, waiting for transfers between devices, shards(): lax.psum_scatter(grad_two, ('face', 'member'), scatter_dimension=0, tiled...  102 us
    unnamed x8, waiting for transfers between devices  77 us
    all_gather x1, blocking collectives, shards(): lax.all_gather(head_weight, ('face', 'member'), axis=0, tiled=True)  67 us
    dot_general x9, matrix products, transpose_conv(): lax.dot_general(flat_slope, weight[tap_index * channels:(tap_index + 1) *...  43.1 us
    all_gather x1, waiting for transfers between devices, shards(): lax.all_gather(conv_weights, ('face', 'member'), axis=0, tiled=True)  36.2 us
    all_gather x1, waiting for transfers between devices, shards(): lax.all_gather(split_edges(features), 'face', axis=1, tiled=True)  32.6 us
  transfers between devices with their start and end apart: 9, of which 8 were waited for; matrix products, arithmetic and copies ran while one was open for 11% of the time, Pallas kernels for 0%

commit v1 on v0

--- a/solution.py
+++ b/solution.py
@@ -4,6 +4,26 @@
 from jax.sharding import PartitionSpec as P
 
 smooth_sq = 0.0625
+
+
+def unite_windows(arr, dim_i):
+    y2, back, q_next = (
+        lax.axis_size(("face", "member")),
+        lax.axis_index(("face", "member")),
+        arr.shape[dim_i],
+    )
+    taken_in, view_out = (arr, 1)
+    while view_out < y2:
+        seen = []
+        pp = 0
+        while pp < y2:
+            seen.append((pp, (pp - view_out) % y2))
+            pp += 1
+        taken_in = jnp.concatenate(
+            [taken_in, lax.ppermute(taken_in, ("face", "member"), seen)], dim_i
+        )
+        view_out = 2 * view_out
+    return jnp.roll(taken_in, back * q_next, dim_i)
 
 
 def split_edges(grid_field):
@@ -151,7 +171,7 @@
     members, tile_dev, height, tile_w, channels = features.shape
     full_weights, full_head = (
         lax.all_gather(conv_weights, ("face", "member"), axis=0, tiled=True),
-        lax.all_gather(head_weight, ("face", "member"), axis=0, tiled=True),
+        unite_windows(head_weight, 0),
     )
     selector, flip_flags = partner_table(
         adjacency, placement_map, lax.axis_index("face") * tile_dev, tile_dev

time: 861 us -> 833 us (0.967)
  blocking collectives: 67 us -> 0 us
  waiting for transfers between devices: 396 us -> 426 us
    all_gather x1 -> x0, blocking collectives: 67 us -> none  [shards(): lax.all_gather(head_weight, ('face', 'member'), axis=0, tiled=True)]
    ppermute x0 -> x5, waiting for transfers between devices: none -> 12.6 us  [unite_windows(): lax.ppermute(taken_in, ('face', 'member'), seen)]
    all_gather x1, waiting for transfers between devices: 0.01 us -> 12 us  [shards(): lax.all_gather(split_edges(act_one), 'face', axis=1, tiled=True)]
  transfers between devices with their start and end apart: 9 -> 14, of which waited for: 8 -> 14; matrix products, arithmetic and copies ran while one was open for 11% -> 12% of each run, Pallas kernels for 0% -> 0%
where the time goes in v1:
time: 833 us; the launch traced here: 822 us
  waiting for transfers between devices  426 us (51%)
  local copies, waits for them, and re-layouts  218 us (26%)
  matrix products  101 us (12%)
  other arithmetic  46.1 us (6%)
  between operations  15.6 us (2%)
  starting transfers between devices  15.3 us (2%)
    scatter-add x9, local copies, waits for them, and re-layouts, transpose_conv(): result.at[:, :, row_off:row_off + height, col_off:col_off + tile_w, :]  141 us
    reduce_scatter x1, waiting for transfers between devices, shards(): lax.psum_scatter(grad_one, ('face', 'member'), scatter_dimension=0, tiled...  104 us
    reduce_scatter x1, waiting for transfers between devices, shards(): lax.psum_scatter(grad_two, ('face', 'member'), scatter_dimension=0, tiled...  102 us
    unnamed x8, waiting for transfers between devices  77 us
    dot_general x9, matrix products, transpose_conv(): lax.dot_general(flat_slope, weight[tap_index * channels:(tap_index + 1) *...  43 us
    all_gather x1, waiting for transfers between devices, shards(): lax.all_gather(conv_weights, ('face', 'member'), axis=0, tiled=True)  36.2 us
    all_gather x1, waiting for transfers between devices, shards(): lax.all_gather(split_edges(features), 'face', axis=1, tiled=True)  32.6 us
    dot_general x18, matrix products, convolve(): jnp.dot(window.reshape(-1, channels), weight[tap_index * channels:(tap_in...  22.1 us
  transfers between devices with their start and end apart: 14, of which 14 were waited for; matrix products, arithmetic and copies ran while one was open for 12% of the time, Pallas kernels for 0%

profile of v1, /device:TPU:0, one launch (start us, length us, event | category | flops | bytes accessed | tf_op | source)
XLA Modules:
  0.0 822.0 jit_solution(10013245279261809047)
XLA Ops:
  13.3 32.6 %all-gather.5.cloned.1.call-done = bf16[2,48,4,16,256]{4,3,1,0,2:T(8,128)(2,1)} async-done(((bf16[2,6,4,16,256]{4,3,1,0,2:T(8,128)(2,1)}), bf16[2,48,4,16,256]{4,3,1,0,2:T(8,128)(2,1)}) %all-gather.5.cloned.1.call-update) | async-done | bytes 3145744 | tf_op jit(solution)/shard_map/all_gather | solution.py:179
  45.9 2.3 copy.341
  48.3 3.4 reshape.811
  51.7 2.6 fusion.3
  57.0 3.0 pad_maximum_fusion.4
  60.0 3.6 pad_maximum_fusion
  63.6 3.7 fusion.112
  67.3 3.2 fusion.111
  70.5 36.2 %all-gather.7.cloned.1.call-done = bf16[2304,2,256]{2,0,1:T(8,128)(2,1)} async-done(((bf16[72,2,256]{2,0,1:T(8,128)(2,1)}), bf16[2304,2,256]{2,0,1:T(8,128)(2,1)}) %all-gather.7.cloned.1.call-update) | async-done | bytes 2359312 | tf_op jit(solution)/shard_map/all_gather | solution.py:173
  106.7 2.1 fusion.32
  124.5 2.9 collective-permute-start
  129.0 4.8 collective-permute-done.1
  133.9 1.8 collective-permute-done.2
  137.3 2.2 collective-permute-done.3
  141.3 2.3 collective-permute-done.4
  143.7 12.0 %all-gather.9.cloned.1.call-done = bf16[2,48,4,16,256]{4,3,2,1,0:T(8,128)(2,1)} async-done(((bf16[2,6,4,16,256]{4,3,2,1,0:T(8,128)(2,1)}), bf16[2,48,4,16,256]{4,3,2,1,0:T(8,128)(2,1)}) %all-gather.9.cloned.1.call-update) | async-done | bytes 3145744 | tf_op jit(solution)/shard_map/all_gather | solution.py:183
  155.7 6.1 reshape.813
  161.8 2.6 fusion.4
  168.7 3.9 pad_maximum_fusion.1
  182.5 2.4 convolution_add_fusion
  184.9 3.5 copy.375
  188.4 3.9 multiply_convert_fusion.2
  192.3 1.9 fusion.10
  194.2 1.9 copy.377
  196.1 5.0 all-to-all-start
  201.2 20.5 %all-to-all-done = bf16[2,6,80,256]{2,0,1,3:T(2,128)(2,1)S(1)} async-done(((bf16[2,6,80,256]{2,0,1,3:T(2,128)(2,1)}), bf16[2,6,80,256]{2,0,1,3:T(2,128)(2,1)S(1)}, u32[]{:S(2)}, u32[]{:S(2)}) %all-to-all-start) | async-done | bytes 491552 | tf_op jit(solution)/shard_map/all_to_all | solution.py:191
  222.1 3.1 fusion.2
  226.6 3.5 all-to-all-start.1
  232.3 17.4 %all-to-all-done.1 = bf16[8,6,80,64]{2,3,1,0:T(8,128)(2,1)S(1)} async-done(((bf16[8,6,80,64]{2,3,1,0:T(8,128)(2,1)}), bf16[8,6,80,64]{2,3,1,0:T(8,128)(2,1)S(1)}, u32[]{:S(2)}, u32[]{:S(2)}) %all-to-all-start.1) | async-done | bytes 491552 | tf_op jit(solution)/shard_map/all_to_all | solution.py:196
  249.9 3.5 multiply_convert_fusion.1
  256.3 3.0 scatter-add.44
  259.3 4.8 dynamic-slice_add_fusion
  264.1 18.3 %scatter-add.45 = f32[2,6,18,18,256]{4,2,3,1,0:T(8,128)} dynamic-update-slice(f32[2,6,18,18,256]{4,2,3,1,0:T(8,128)} %scatter-add.44, f32[2,6,16,16,256]{4,2,3,1,0:T(8,128)} %dynamic-slice_add_fusion, s32[]{:T(128)} %constant.416.clone.1, s32[]{:T(128)} %constant.416.clone.1, s32[]{:T(128)} %bitcast.74, s32[]{:T(128)} %bitcast.75, s32[]{:T(128)} %constant.416.clone.1) | dynamic-update-slice | bytes 6291460 | tf_op jit(solution)/shard_map/scatter-add | solution.py:96
  282.3 6.9 add_select_fusion
  289.2 18.2 %scatter-add.46 = f32[2,6,18,18,256]{4,2,3,1,0:T(8,128)} dynamic-update-slice(f32[2,6,18,18,256]{4,2,3,1,0:T(8,128)} %scatter-add.45, f32[2,6,16,16,256]{4,2,3,1,0:T(8,128)} %add_select_fusion, s32[]{:T(128)} %constant.416.clone.1, s32[]{:T(128)} %constant.416.clone.1, s32[]{:T(128)} %bitcast.78, s32[]{:T(128)} %bitcast.79, s32[]{:T(128)} %constant.416.clone.1) | dynamic-update-slice | bytes 6291460 | tf_op jit(solution)/shard_map/scatter-add | solution.py:96
  307.4 4.9 slice_add_fusion.5
  312.3 17.0 %scatter-add.49 = f32[2,6,18,18,256]{4,2,3,1,0:T(8,128)} dynamic-update-slice(f32[2,6,18,18,256]{4,2,3,1,0:T(8,128)} %scatter-add.46, f32[2,6,16,16,256]{4,2,3,1,0:T(8,128)} %slice_add_fusion.5, s32[]{:T(128)} %constant.416.clone.1, s32[]{:T(128)} %constant.416.clone.1, s32[]{:T(128)} %constant.417.clone.1, s32[]{:T(128)} %constant.416.clone.1, s32[]{:T(128)} %constant.416.clone.1) | dynamic-update-slice | bytes 6291460 | tf_op jit(solution)/shard_map/scatter-add | solution.py:96
  329.3 5.0 slice_add_fusion.4
  334.2 16.9 %scatter-add.50 = f32[2,6,18,18,256]{4,2,3,1,0:T(8,128)} dynamic-update-slice(f32[2,6,18,18,256]{4,2,3,1,0:T(8,128)} %scatter-add.49, f32[2,6,16,16,256]{4,2,3,1,0:T(8,128)} %slice_add_fusion.4, s32[]{:T(128)} %constant.416.clone.1, s32[]{:T(128)} %constant.416.clone.1, s32[]{:T(128)} %constant.417.clone.1, s32[]{:T(128)} %constant.417.clone.1, s32[]{:T(128)} %constant.416.clone.1) | dynamic-update-slice | bytes 6291460 | tf_op jit(solution)/shard_map/scatter-add | solution.py:96
  351.2 5.0 slice_add_fusion.3
  356.1 16.9 %scatter-add.51 = f32[2,6,18,18,256]{4,2,3,1,0:T(8,128)} dynamic-update-slice(f32[2,6,18,18,256]{4,2,3,1,0:T(8,128)} %scatter-add.50, f32[2,6,16,16,256]{4,2,3,1,0:T(8,128)} %slice_add_fusion.3, s32[]{:T(128)} %constant.416.clone.1, s32[]{:T(128)} %constant.416.clone.1, s32[]{:T(128)} %constant.417.clone.1, s32[]{:T(128)} %constant.430.clone.1, s32[]{:T(128)} %constant.416.clone.1) | dynamic-update-slice | bytes 6291460 | tf_op jit(solution)/shard_map/scatter-add | solution.py:96
  373.1 5.0 slice_add_fusion.2
  378.0 17.0 %scatter-add.54 = f32[2,6,18,18,256]{4,2,3,1,0:T(8,128)} dynamic-update-slice(f32[2,6,18,18,256]{4,2,3,1,0:T(8,128)} %scatter-add.51, f32[2,6,16,16,256]{4,2,3,1,0:T(8,128)} %slice_add_fusion.2, s32[]{:T(128)} %constant.416.clone.1, s32[]{:T(128)} %constant.416.clone.1, s32[]{:T(128)} %constant.430.clone.1, s32[]{:T(128)} %constant.416.clone.1, s32[]{:T(128)} %constant.416.clone.1) | dynamic-update-slice | bytes 6291460 | tf_op jit(solution)/shard_map/scatter-add | solution.py:96
  395.0 5.0 slice_add_fusion.1
  399.9 16.9 %scatter-add.55 = f32[2,6,18,18,256]{4,2,3,1,0:T(8,128)} dynamic-update-slice(f32[2,6,18,18,256]{4,2,3,1,0:T(8,128)} %scatter-add.54, f32[2,6,16,16,256]{4,2,3,1,0:T(8,128)} %slice_add_fusion.1, s32[]{:T(128)} %constant.416.clone.1, s32[]{:T(128)} %constant.416.clone.1, s32[]{:T(128)} %constant.430.clone.1, s32[]{:T(128)} %constant.417.clone.1, s32[]{:T(128)} %constant.416.clone.1) | dynamic-update-slice | bytes 6291460 | tf_op jit(solution)/shard_map/scatter-add | solution.py:96
  416.9 4.9 slice_add_fusion
  421.8 16.9 %scatter-add.56 = f32[2,6,18,18,256]{4,2,3,1,0:T(8,128)} dynamic-update-slice(f32[2,6,18,18,256]{4,2,3,1,0:T(8,128)} %scatter-add.55, f32[2,6,16,16,256]{4,2,3,1,0:T(8,128)} %slice_add_fusion, s32[]{:T(128)} %constant.416.clone.1, s32[]{:T(128)} %constant.416.clone.1, s32[]{:T(128)} %constant.430.clone.1, s32[]{:T(128)} %constant.430.clone.1, s32[]{:T(128)} %constant.416.clone.1) | dynamic-update-slice | bytes 6291460 | tf_op jit(solution)/shard_map/scatter-add | solution.py:96
  438.8 2.9 convert_element_type.103
  444.7 2.8 convolution_bitcast_fusion.18
  447.5 3.2 fusion.17
  459.2 3.9 slice_convert_fusion
  463.2 11.6 %all-gather.11.cloned.1.call-done = bf16[2,48,4,16,256]{4,3,1,0,2:T(8,128)(2,1)} async-done(((bf16[2,6,4,16,256]{4,3,1,0,2:T(8,128)(2,1)}), bf16[2,48,4,16,256]{4,3,1,0,2:T(8,128)(2,1)}) %all-gather.11.cloned.1.call-update) | async-done | bytes 3145744 | tf_op jit(solution)/shard_map/all_gather | solution.py:207
  474.8 2.3 copy.393
  477.2 3.4 reshape.825
  480.6 2.6 fusion.5
  484.4 2.1 fusion.116
  486.5 5.5 scatter-add.59
  495.3 5.5 scatter-add.61
  500.7 5.9 copy.399
  509.1 5.7 scatter-add.64
  514.8 3.1 multiply_convert_fusion
  528.4 76.9 %all-reduce.4.cloned.1.call-done = f32[256,80]{1,0:T(8,128)} async-done(((f32[256,80]{1,0:T(8,128)}), f32[256,80]{1,0:T(8,128)}) %all-reduce.4.cloned.1.call-update) | async-done | bytes 81936
  606.6 102.5 %reduce-scatter.5.cloned.1.call-done = f32[72,256]{1,0:T(8,128)} async-done(((f32[2304,256]{1,0:T(8,128)}), f32[72,256]{1,0:T(8,128)}) %reduce-scatter.5.cloned.1.call-update) | async-done | bytes 73744 | tf_op jit(solution)/shard_map/reduce_scatter | solution.py:203
  709.1 103.9 %reduce-scatter.3.cloned.1.call-done = f32[72,256]{1,0:T(8,128)} async-done(((f32[2304,256]{1,0:T(8,128)}), f32[72,256]{1,0:T(8,128)}) %reduce-scatter.3.cloned.1.call-update) | async-done | bytes 73744 | tf_op jit(solution)/shard_map/reduce_scatter | solution.py:216
  (206 shorter events, 82.0 us)
Async XLA Ops:
  7.2 3.7 copy-start.33
  7.2 4.5 copy-start.37
  7.2 4.7 copy-start.34
  7.2 38.7 %all-gather.5.cloned.1.call-start = ((), (), s32[]{:S(2)}) async-start(), calls=%async_computation.4 | async-start | bytes 3538944 | tf_op jit(solution)/shard_map/all_gather | solution.py:179
  10.8 95.9 %all-gather.7.cloned.1.call-start = ((), (), s32[]{:S(2)}) async-start(), calls=%async_computation.5 | async-start | bytes 2433024 | tf_op jit(solution)/shard_map/all_gather | solution.py:173
  11.6 144.1 %all-gather.9.cloned.1.call-start = ((), (), s32[]{:S(2)}) async-start(), calls=%async_computation.6 | async-start | bytes 3538944 | tf_op jit(solution)/shard_map/all_gather | solution.py:183
  54.8 2.2 copy-start.12
  60.0 55.0 %copy-start.14 = (bf16[2,6,16,16,256]{4,3,2,1,0:T(8,128)(2,1)}, bf16[2,6,16,16,256]{4,3,2,1,0:T(8,128)(2,1)S(1)}, u32[]{:S(2)}) copy-start(bf16[2,6,16,16,256]{4,3,2,1,0:T(8,128)(2,1)S(1)} %get-tuple-element.196) | copy-start | bytes 4718596
  63.6 3.7 copy-start.7
  63.6 3.7 copy-start
  106.7 2.1 copy-start.27
  108.8 1.6 copy-start.26
  110.4 1.6 copy-start.16
  115.0 1.6 copy-start.25
  116.6 1.6 copy-start.24
  118.3 1.6 copy-start.23
  121.4 1.6 copy-start.4
  123.0 1.3 copy-start.35
  124.5 4.4 collective-permute-start
  128.9 4.8 collective-permute-start.1
  133.8 1.9 collective-permute-start.2
  135.8 3.8 collective-permute-start.3
  139.7 3.8 collective-permute-start.4
  168.7 9.1 %copy-start.20 = (bf16[2,6,16,16,256]{4,3,2,1,0:T(8,128)(2,1)}, bf16[2,6,16,16,256]{4,3,2,1,0:T(8,128)(2,1)S(1)}, u32[]{:S(2)}) copy-start(bf16[2,6,16,16,256]{4,3,2,1,0:T(8,128)(2,1)S(1)} %get-tuple-element.191) | copy-start | bytes 4718596
  168.7 11.9 %copy-start.18 = (bf16[2,6,16,16,256]{4,3,2,1,0:T(8,128)(2,1)}, bf16[2,6,16,16,256]{4,3,2,1,0:T(8,128)(2,1)S(1)}, u32[]{:S(2)}) copy-start(bf16[2,6,16,16,256]{4,3,2,1,0:T(8,128)(2,1)S(1)} %get-tuple-element.190) | copy-start | bytes 4718596
  172.6 1.5 copy-start.2
  172.6 2.7 copy-start.9
  174.1 1.9 copy-start.28
  177.8 1.9 copy-start.5
  192.3 8.8 %copy-start.32 = (bf16[6,80,64]{1,2,0:T(8,128)(2,1)S(1)}, bf16[6,80,64]{1,2,0:T(8,128)(2,1)}, u32[]{:S(2)}) copy-start(bf16[6,80,64]{1,2,0:T(8,128)(2,1)} %param.33) | copy-start | bytes 184324
  196.1 25.6 %all-to-all-start = ((bf16[2,6,80,256]{2,0,1,3:T(2,128)(2,1)}), bf16[2,6,80,256]{2,0,1,3:T(2,128)(2,1)S(1)}, u32[]{:S(2)}, u32[]{:S(2)}) async-start(bf16[2,6,80,256]{2,0,1,3:T(2,128)(2,1)} %copy.377), calls=%async_computation | async-start | bytes 1572864 | tf_op jit(solution)/shard_map/all_to_all | solution.py:191
  225.2 6.4 copy-start.36
  226.6 23.1 %all-to-all-start.1 = ((bf16[8,6,80,64]{2,3,1,0:T(8,128)(2,1)}), bf16[8,6,80,64]{2,3,1,0:T(8,128)(2,1)S(1)}, u32[]{:S(2)}, u32[]{:S(2)}) async-start(bf16[8,6,80,64]{2,3,1,0:T(8,128)(2,1)} %multiply_convert_fusion.6), calls=%async_computation.1 | async-start | bytes 1572864 | tf_op jit(solution)/shard_map/all_to_all | solution.py:196
  230.1 244.7 %all-gather.11.cloned.1.call-start = ((), (), s32[]{:S(2)}) async-start(), calls=%async_computation.7 | async-start | bytes 3538944 | tf_op jit(solution)/shard_map/all_gather | solution.py:207
  249.8 3.6 copy-start.29
  249.8 3.6 copy-start.10
  438.8 3.4 copy-start.11
  441.7 1.9 copy-start.22
  444.4 160.9 %all-reduce.4.cloned.1.call-start = ((), (), s32[]{:S(2)}) async-start(), calls=%async_computation.10 | async-start | bytes 262144
  447.5 3.2 copy-start.21
  452.0 1.4 copy-start.19
  453.4 1.8 copy-start.3
  459.2 249.9 %reduce-scatter.5.cloned.1.call-start = ((), (), s32[]{:S(2)}) async-start(), calls=%async_computation.9 | async-start | bytes 2433024 | tf_op jit(solution)/shard_map/reduce_scatter | solution.py:203
  463.2 349.9 %reduce-scatter.3.cloned.1.call-start = ((), (), s32[]{:S(2)}) async-start(), calls=%async_computation.8 | async-start | bytes 2433024 | tf_op jit(solution)/shard_map/reduce_scatter | solution.py:216
  484.3 10.9 %copy-start.30 = (f32[2,6,4,16,256]{4,2,3,1,0:T(4,128)}, f32[2,6,4,16,256]{4,2,3,1,0:T(4,128)S(1)}, u32[]{:S(2)}) copy-start(f32[2,6,4,16,256]{4,2,3,1,0:T(4,128)S(1)} %fusion.29) | copy-start | bytes 2359300
  500.7 14.0 %copy-start.6 = (f32[3072,256]{1,0:T(8,128)S(1)}, f32[3072,256]{1,0:T(8,128)}, u32[]{:S(2)}) copy-start(f32[3072,256]{1,0:T(8,128)} %copy-done.4) | copy-start | bytes 9437188
  514.8 3.1 copy-start.8
  519.1 1.4 copy-start.17
  520.6 1.4 copy-start.13
  522.0 1.4 copy-start.15
  523.4 1.7 copy-start.1
  527.0 1.4 copy-start.31
Sparse Core Ops, SparseCore 0:
  11.0 34.8 all-gather.4
  49.5 57.1 all-gather.6
  124.5 31.2 all-gather.8
  444.5 30.2 all-gather.10
  480.8 124.4 all-reduce.3
  610.5 98.5 reduce-scatter.4
  714.4 98.6 reduce-scatter.2
